TPU v7x, 512 devices: a whole 4x4x16 slice. The times are simulated.
512 devices in a mesh: dp: 4 (over x), cand: 32 (over z, core), tensor: 4 (over y).
Axes of the slice: x: 4, y: 4, z: 16, core: 2. Of those that a mesh axis runs over, the one named last changes fastest.
Arguments:
- context: bfloat16 [8, 4096, 3584], P('dp', 'cand', 'tensor'), may hold values from -12 to 12
- residual: bfloat16 [8, 4096, 3584], P('dp', ('cand', 'tensor')), may hold values from -36 to 36
- out_weight: bfloat16 [3584, 3584], P('cand', 'tensor'), may hold values from -0.09375 to 0.09375
- adapter_down: bfloat16 [3584, 16], P('tensor'), may hold values from -0.09375 to 0.09375
- adapter_up_weight: bfloat16 [16, 3584], replicated, may hold values from -1.5 to 1.5
- norm_gain: float32 [3584], replicated, may hold values from 0.5 to 1.5
- score_weight: float32 [3584], replicated, may hold values from -0.09375 to 0.09375
- teacher: bfloat16 [8, 4096, 4096], P('dp', 'cand', 'tensor'), may hold values from 0.019897461 to 0.9765625
- pair_mask: int32 [8, 4096, 4096], P('dp', 'cand', 'tensor'), may hold values from 0 to 1, as said below
- loss_scale: float32 [8], P('dp'), may hold values from 65536 to 262144
Outputs:
- context_grad: bfloat16 [8, 4096, 3584], P('dp', 'cand', 'tensor')
- residual_gradient: bfloat16 [8, 4096, 3584], P('dp', ('cand', 'tensor'))
- down_grad: float32 [3584, 16], P('tensor')
- up_weight_gradient: float32 [16, 3584], P(None, 'tensor')
- pair_loss: float32 [8], P('dp')
Inputs may be any that keep to these rules, and one draw needn't show every extreme that they name: pair_mask holds 0 or 1; with P = 32, every pair (i, j) whose group j // P lies 4096 / (2P) groups after i // P, counted round over the 4096 / P groups, is valid.
All inputs are finite; a program needn't handle non-finite values.
Results may differ from a plain program's by a relative error of at most 0.02.
Values may be sent and summed in bfloat16 or wider, within the bound.
No kernel may reach another device: no remote copies, remote signals or barrier semaphores. Data moves between devices by JAX's collectives and lax.ppermute only.
A program may use at most 64 MiB of HBM per device.

v0:
```python
import jax
import jax.numpy as jnp
from jax import lax
from jax.sharding import PartitionSpec as P

ADAPTER_SCALE = 0.5
epsilon = 1e-06


def rounded(term):
    return lax.optimization_barrier(term.astype(jnp.bfloat16)).astype(jnp.float32)


def pair_terms(all_scores, own_scores, teacher, valid_pairs, row_start, col_start):
    column_scores = lax.dynamic_slice_in_dim(all_scores, col_start, teacher.shape[2], 1)
    margin = own_scores[:, :, None] - column_scores[:, None, :]
    target = teacher.astype(jnp.float32)
    total = jnp.sum(valid_pairs * (jax.nn.softplus(margin) - target * margin), axis=(1, 2))
    slope = valid_pairs * (jax.nn.sigmoid(margin) - target)
    blank = jnp.zeros(all_scores.shape, jnp.float32)
    row_part = lax.dynamic_update_slice_in_dim(blank, jnp.sum(slope, axis=2), row_start, 1)
    column_part = lax.dynamic_update_slice_in_dim(blank, jnp.sum(slope, axis=1), col_start, 1)
    return (total, row_part - column_part)


def on_device(
    context,
    residual,
    out_weight,
    adapter_down,
    adapter_up_weight,
    norm_gain,
    score_weight,
    teacher,
    pair_mask,
    loss_scale,
):
    cand_rows = context.shape[1]
    tensor_count = lax.axis_size("tensor")
    share = cand_rows // tensor_count
    tensor_index = lax.axis_index("tensor")
    group_index = lax.axis_index("cand")
    valid_pairs = pair_mask.astype(jnp.float32)
    mask_count = jnp.sum(valid_pairs, axis=(1, 2))
    count = lax.psum(mask_count, ("cand", "tensor"))
    low_terms = rounded(
        jnp.einsum("qch,hr->qcr", context, adapter_down, preferred_element_type=jnp.float32)
    )
    full_weight = lax.all_gather(out_weight, "cand", axis=0, tiled=True)
    head_terms = jnp.einsum("qch,dh->qcd", context, full_weight, preferred_element_type=jnp.float32)
    head_terms = rounded(head_terms)
    summed_output, low_sum = (
        lax.psum_scatter(
            head_terms.astype(jnp.bfloat16), "tensor", scatter_dimension=1, tiled=True
        ).astype(jnp.float32),
        lax.psum_scatter(
            low_terms.astype(jnp.bfloat16), "tensor", scatter_dimension=1, tiled=True
        ).astype(jnp.float32),
    )
    adapter_input_rows = low_sum.astype(jnp.bfloat16)
    lifted_rows = jnp.einsum(
        "qcr,rd->qcd", adapter_input_rows, adapter_up_weight, preferred_element_type=jnp.float32
    )
    hidden_state = (
        residual.astype(jnp.float32) + summed_output + ADAPTER_SCALE * lifted_rows
    ).astype(jnp.bfloat16)
    hidden_wide = hidden_state.astype(jnp.float32)
    inv_rms = lax.rsqrt(jnp.mean(hidden_wide * hidden_wide, axis=2, keepdims=True) + epsilon)
    scores = jnp.sum(hidden_wide * inv_rms * norm_gain * score_weight, axis=2)
    all_scores = lax.all_gather(scores, ("cand", "tensor"), axis=1, tiled=True)
    own_start = group_index * cand_rows + tensor_index * share
    row_start = group_index * cand_rows
    col_start = tensor_index * teacher.shape[2]
    own_scores = lax.dynamic_slice_in_dim(all_scores, row_start, cand_rows, 1)
    total, score_vector = pair_terms(
        all_scores, own_scores, teacher, valid_pairs, row_start, col_start
    )
    summed_grad, loss_sum = lax.psum((score_vector, total), ("cand", "tensor"))
    pair_loss = loss_sum / count
    factor = loss_scale / count
    score_grad = lax.dynamic_slice_in_dim(summed_grad, own_start, share, 1) * factor[:, None]
    back_step = score_grad[:, :, None] * norm_gain * score_weight
    grad_hidden = inv_rms * back_step - hidden_wide * inv_rms**3 * jnp.mean(
        hidden_wide * back_step, axis=2, keepdims=True
    )
    grad_rows = grad_hidden.astype(jnp.bfloat16)
    adapter_rows = (
        ADAPTER_SCALE
        * jnp.einsum(
            "qcd,rd->qcr", grad_rows, adapter_up_weight, preferred_element_type=jnp.float32
        )
    ).astype(jnp.bfloat16)
    full_grads, full_adapter = (
        lax.all_gather(grad_rows, "tensor", axis=1, tiled=True),
        lax.all_gather(adapter_rows, "tensor", axis=1, tiled=True),
    )
    up_partial_gradient = ADAPTER_SCALE * jnp.einsum(
        "qcr,qcd->rd", adapter_input_rows, grad_rows, preferred_element_type=jnp.float32
    )
    up_share = lax.psum_scatter(
        up_partial_gradient.astype(jnp.bfloat16), "tensor", scatter_dimension=1, tiled=True
    ).astype(jnp.float32)
    adapter_back = jnp.einsum(
        "qcr,hr->qch", full_adapter, adapter_down, preferred_element_type=jnp.float32
    )
    context_wide = (
        jnp.einsum("qcd,dh->qch", full_grads, full_weight, preferred_element_type=jnp.float32)
        + adapter_back
    )
    context_grad = context_wide.astype(jnp.bfloat16)
    down_local = jnp.einsum(
        "qch,qcr->hr", context, full_adapter, preferred_element_type=jnp.float32
    )
    down_grad, up_weight_gradient = lax.psum((down_local, up_share), ("dp", "cand"))
    return (context_grad, grad_rows, down_grad, up_weight_gradient, pair_loss)


def solution(mesh):
    in_specs = (
        P("dp", "cand", "tensor"),
        P("dp", ("cand", "tensor"), None),
        P("cand", "tensor"),
        P("tensor", None),
        P(),
        P(),
        P(),
        P("dp", "cand", "tensor"),
        P("dp", "cand", "tensor"),
        P("dp"),
    )
    out_specs = (
        P("dp", "cand", "tensor"),
        P("dp", ("cand", "tensor"), None),
        P("tensor", None),
        P(None, "tensor"),
        P("dp"),
    )
    return jax.shard_map(
        on_device, mesh=mesh, in_specs=in_specs, out_specs=out_specs, check_vma=False
    )
```

profile of v0, /device:TPU:16, one launch (start us, length us, event | category | flops | bytes accessed | tf_op | source)
XLA Modules:
  0.0 1309.3 jit_solution(4041656282521602248)
XLA Ops:
  8.1 0.7 all-gather.4.cloned.1.call-update
  8.8 0.2 copy-done
  9.0 0.9 convolution_convert_fusion
  10.0 0.2 copy.20
  10.2 0.7 reshape.41
  11.0 81.7 %all-gather.4.cloned.1.call-done = bf16[3584,896]{1,0:T(8,128)(2,1)} async-done(((bf16[112,896]{1,0:T(8,128)(2,1)}), bf16[3584,896]{1,0:T(8,128)(2,1)}) %all-gather.4.cloned.1.call-update) | async-done | bytes 6422544 | tf_op jit(solution)/shard_map/all_gather | solution.py:49
  92.7 6.2 fusion.4
  99.0 0.8 reshape.42
  99.8 0.7 copy.21
  100.4 29.0 %reduce-scatter.8.cloned.1.call-done = bf16[2,32,3584]{2,1,0:T(8,128)(2,1)} async-done(((bf16[2,128,3584]{2,1,0:T(8,128)(2,1)}), bf16[2,32,3584]{2,1,0:T(8,128)(2,1)}) %reduce-scatter.8.cloned.1.call-update) | async-done | bytes 458768 | tf_op jit(solution)/shard_map/reduce_scatter | solution.py:53
  129.5 1.5 multiply_reduce_fusion.2
  131.0 0.3 multiply_reduce_fusion.1
  131.3 140.3 %all-gather = f32[128,32,2]{1,2,0:T(2,128)S(1)} all-gather(f32[1,32,2]{1,2,0:T(2,128)S(1)} %bitcast.57), channel_id=1, replica_groups=mesh['dp'=4,'cand'=32,'tensor'=4] {'cand','tensor'}, dimensions={0}, use_global_device_ids=true | all-gather | bytes 33024 | tf_op jit(solution)/shard_map/all_gather | solution.py:70
  271.6 0.1 reshape.35
  271.8 1.2 fusion.24
  273.0 0.2 fusion.31
  273.3 493.2 %all-reduce = (f32[2,4096]{1,0:T(2,128)S(1)}, f32[2]{0:T(128)S(1)}, f32[2]{0:T(128)S(1)}) all-reduce(f32[2,4096]{1,0:T(2,128)S(1)} %sub.29, f32[2]{0:T(128)S(1)} %get-tuple-element.6, f32[2]{0:T(128)S(1)} %get-tuple-element.5), channel_id=1, replica_groups=mesh['dp'=4,'cand'=32,'tensor'=4] {'cand','tensor'}, use_global_device_ids=true, to_apply=%region_6.7 | all-reduce | flops 8196 | bytes 65568 | tf_op jit(solution)/shard_map/psum | solution.py:78
  766.4 1.2 fusion.32
  767.7 0.3 multiply_reduce_fusion
  768.0 0.3 subtract_convert_fusion
  768.3 0.2 fusion.11
  768.5 1.3 copy.22
  769.9 0.7 all-gather.6.cloned.1.call-update
  770.6 1.4 fusion.13
  772.0 0.1 copy.17
  772.1 13.7 %all_gather.15 = bf16[2,128,16]{2,0,1:T(2,128)(2,1)S(1)} all-gather(bf16[2,32,16]{2,0,1:T(2,128)(2,1)S(1)} %copy.17), channel_id=1, replica_groups=mesh['dp'=4,'cand'=32,'tensor'=4] {'tensor'}, dimensions={1}, use_global_device_ids=true | all-gather | bytes 10240 | tf_op jit(solution)/shard_map/all_gather | solution.py:95
  785.9 0.2 convolution_bitcast_fusion.1
  786.1 13.0 reduce-scatter.12.cloned.1.call-done
  799.1 1.0 copy.23
  800.1 495.1 %all-reduce.3 = (f32[896,16]{0,1:T(8,128)}, f32[16,896]{1,0:T(8,128)}) all-reduce(f32[896,16]{0,1:T(8,128)S(1)} %convolution_bitcast_fusion.1, bf16[16,896]{1,0:T(8,128)(2,1)S(1)} %copy.23), channel_id=1, replica_groups=mesh['dp'=4,'cand'=32,'tensor'=4] {'dp','cand'}, use_global_device_ids=true, to_apply=%region_10.11 | all-reduce | flops 28672 | bytes 200704 | tf_op jit(solution)/shard_map/psum | solution.py:114
  1295.2 5.5 fusion
  1300.6 1.1 fusion.12
  (41 shorter events, 0.6 us)
Async XLA Ops:
  8.0 1.0 copy-start
  8.0 84.7 %all-gather.4.cloned.1.call-start = ((), (), s32[]{:S(2)}) async-start(), calls=%async_computation.3 | async-start | bytes 6623232 | tf_op jit(solution)/shard_map/all_gather | solution.py:49
  8.7 90.2 %reduce-scatter.10.cloned.1.call-start = ((), (), s32[]{:S(2)}) async-start(), calls=%async_computation.6 | async-start | bytes 40960
  10.9 118.6 %copy-start.4 = (bf16[2,32,3584]{2,1,0:T(8,128)(2,1)S(1)}, bf16[2,32,3584]{2,1,0:T(8,128)(2,1)}, u32[]{:S(2)}) copy-start(bf16[2,32,3584]{2,1,0:T(8,128)(2,1)} %param.11) | copy-start | bytes 1376260
  10.9 118.6 %copy-start.5 = (bf16[16,3584]{1,0:T(8,128)(2,1)S(1)}, bf16[16,3584]{1,0:T(8,128)(2,1)}, u32[]{:S(2)}) copy-start(bf16[16,3584]{1,0:T(8,128)(2,1)} %param.14) | copy-start | bytes 344068
  10.9 120.1 %copy-start.6 = (f32[3584]{0:T(1024)S(1)}, f32[3584]{0:T(1024)}, u32[]{:S(2)}) copy-start(f32[3584]{0:T(1024)} %param.16) | copy-start | bytes 43012
  10.9 120.1 %copy-start.7 = (f32[3584]{0:T(1024)S(1)}, f32[3584]{0:T(1024)}, u32[]{:S(2)}) copy-start(f32[3584]{0:T(1024)} %param.15) | copy-start | bytes 43012
  10.9 260.8 %copy-start.2 = (s32[2,128,1024]{2,1,0:T(8,128)S(1)}, s32[2,128,1024]{2,1,0:T(8,128)}, u32[]{:S(2)}) copy-start(s32[2,128,1024]{2,1,0:T(8,128)} %param.18) | copy-start | bytes 3145732
  11.0 260.8 %copy-start.3 = (bf16[2,128,1024]{2,1,0:T(8,128)(2,1)S(1)}, bf16[2,128,1024]{2,1,0:T(8,128)(2,1)}, u32[]{:S(2)}) copy-start(bf16[2,128,1024]{2,1,0:T(8,128)(2,1)} %param.17) | copy-start | bytes 1572868
  11.0 118.5 %reduce-scatter.8.cloned.1.call-start = ((), (), s32[]{:S(2)}) async-start(), calls=%async_computation.4 | async-start | bytes 2293760 | tf_op jit(solution)/shard_map/reduce_scatter | solution.py:53
  98.9 700.2 %reduce-scatter.12.cloned.1.call-start = ((), (), s32[]{:S(2)}) async-start(), calls=%async_computation.7 | async-start | bytes 1146880
  130.9 637.3 %copy-start.9 = (bf16[2,32,16]{1,2,0:T(8,128)(2,1)S(1)}, bf16[2,32,16]{1,2,0:T(8,128)(2,1)}, u32[]{:S(2)}) copy-start(bf16[2,32,16]{1,2,0:T(8,128)(2,1)} %copy.21) | copy-start | bytes 6148
  768.3 1.7 copy-start.1
  769.9 525.3 %all-gather.6.cloned.1.call-start = ((), (), s32[]{:S(2)}) async-start(), calls=%async_computation.5 | async-start | bytes 2293760 | tf_op jit(solution)/shard_map/all_gather | solution.py:94
  1295.2 5.5 copy-start.8
Sparse Core Ops, SparseCore 0:
  11.2 81.4 all-gather.3
Sparse Core Ops, SparseCore 1:
  12.6 30.7 reduce-scatter.9
  99.0 30.5 reduce-scatter.7
  769.9 29.1 reduce-scatter.11
  802.0 36.1 all-gather.5
where the time goes:
time: 1310 us
  blocking collectives  1140 us (87%)
  waiting for transfers between devices  125 us (10%)
  matrix products  16.9 us (1%)
  between operations  15.9 us (1%)
    psum x1, blocking collectives, on_device(): lax.psum((down_local, up_share), ('dp', 'cand'))  495 us
    psum x1, blocking collectives, on_device(): summed_grad, loss_sum = lax.psum((score_vector, total), ('cand', 'tensor'))  493 us
    all_gather x1, blocking collectives, on_device(): all_scores = lax.all_gather(scores, ('cand', 'tensor'), axis=1, tiled=True)  140 us
    all_gather x1, waiting for transfers between devices, on_device(): full_weight = lax.all_gather(out_weight, 'cand', axis=0, tiled=True)  81.7 us
    reduce_scatter x1, waiting for transfers between devices, on_device(): lax.psum_scatter(head_terms.astype(jnp.bfloat16), 'tensor', scatter_dimen...  29 us
  transfers between devices with their start and end apart: 5, of which 3 were waited for; matrix products, arithmetic and copies ran while one was open for 1% of the time, Pallas kernels for 0%

commit v1 on v0

--- a/solution.py
+++ b/solution.py
@@ -111,7 +111,7 @@
     down_local = jnp.einsum(
         "qch,qcr->hr", context, full_adapter, preferred_element_type=jnp.float32
     )
-    down_grad, up_weight_gradient = lax.psum((down_local, up_share), ("dp", "cand"))
+    down_grad, up_weight_gradient = lax.psum(lax.psum((down_local, up_share), "dp"), "cand")
     return (context_grad, grad_rows, down_grad, up_weight_gradient, pair_loss)
 
 

time: 1310 us -> 1020 us (0.78)
  the two profiles are of different devices: /device:TPU:16 before, /device:TPU:1 now
where the time goes in v1:
time: 1020 us
  blocking collectives  655 us (64%)
  waiting for transfers between devices  323 us (32%)
  matrix products  16.9 us (2%)
  between operations  16 us (2%)
    psum x1, blocking collectives, on_device(): summed_grad, loss_sum = lax.psum((score_vector, total), ('cand', 'tensor'))  491 us
    psum x1, waiting for transfers between devices, on_device(): lax.psum(lax.psum((down_local, up_share), 'dp'), 'cand')  165 us
    all_gather x1, blocking collectives, on_device(): all_scores = lax.all_gather(scores, ('cand', 'tensor'), axis=1, tiled=True)  140 us
    all_gather x1, waiting for transfers between devices, on_device(): full_weight = lax.all_gather(out_weight, 'cand', axis=0, tiled=True)  83 us
    reduce_scatter x1, waiting for transfers between devices, on_device(): lax.psum_scatter(head_terms.astype(jnp.bfloat16), 'tensor', scatter_dimen...  30.3 us
    all_gather x1, waiting for transfers between devices, on_device(): lax.all_gather(grad_rows, 'tensor', axis=1, tiled=True)  24.1 us
  transfers between devices with their start and end apart: 6, of which 5 were waited for; matrix products, arithmetic and copies ran while one was open for 2% of the time, Pallas kernels for 0%

profile of v1, /device:TPU:1, one launch (start us, length us, event | category | flops | bytes accessed | tf_op | source)
XLA Modules:
  0.0 1022.7 jit_solution(17939607394888899511)
XLA Ops:
  8.1 0.7 all-gather.4.cloned.1.call-update
  8.8 0.2 copy-done
  9.0 0.9 convolution_convert_fusion
  10.0 0.2 copy.20
  10.2 0.7 reshape.41
  11.0 83.0 %all-gather.4.cloned.1.call-done = bf16[3584,896]{1,0:T(8,128)(2,1)} async-done(((bf16[112,896]{1,0:T(8,128)(2,1)}), bf16[3584,896]{1,0:T(8,128)(2,1)}) %all-gather.4.cloned.1.call-update) | async-done | bytes 6422544 | tf_op jit(solution)/shard_map/all_gather | solution.py:49
  94.0 6.2 fusion.4
  100.3 0.8 reshape.42
  101.0 0.7 copy.21
  101.7 30.3 %reduce-scatter.8.cloned.1.call-done = bf16[2,32,3584]{2,1,0:T(8,128)(2,1)} async-done(((bf16[2,128,3584]{2,1,0:T(8,128)(2,1)}), bf16[2,32,3584]{2,1,0:T(8,128)(2,1)}) %reduce-scatter.8.cloned.1.call-update) | async-done | bytes 458768 | tf_op jit(solution)/shard_map/reduce_scatter | solution.py:53
  132.0 1.5 multiply_reduce_fusion.2
  133.5 0.3 multiply_reduce_fusion.1
  133.8 139.8 %all-gather = f32[128,32,2]{1,2,0:T(2,128)S(1)} all-gather(f32[1,32,2]{1,2,0:T(2,128)S(1)} %bitcast.57), channel_id=1, replica_groups=mesh['dp'=4,'cand'=32,'tensor'=4] {'cand','tensor'}, dimensions={0}, use_global_device_ids=true | all-gather | bytes 33024 | tf_op jit(solution)/shard_map/all_gather | solution.py:70
  273.7 1.2 fusion.24
  275.2 491.3 %all-reduce = (f32[2,4096]{1,0:T(2,128)S(1)}, f32[2]{0:T(128)S(1)}, f32[2]{0:T(128)S(1)}) all-reduce(f32[2,4096]{1,0:T(2,128)S(1)} %sub.29, f32[2]{0:T(128)S(1)} %get-tuple-element.6, f32[2]{0:T(128)S(1)} %get-tuple-element.5), channel_id=1, replica_groups=mesh['dp'=4,'cand'=32,'tensor'=4] {'cand','tensor'}, use_global_device_ids=true, to_apply=%region_6.7 | all-reduce | flops 8196 | bytes 65568 | tf_op jit(solution)/shard_map/psum | solution.py:78
  766.5 1.2 fusion.32
  767.8 0.3 multiply_reduce_fusion
  768.1 0.3 subtract_convert_fusion
  768.4 0.2 fusion.11
  768.6 1.3 copy.22
  770.0 0.7 all-gather.6.cloned.1.call-update
  770.7 1.4 fusion.13
  772.3 9.0 all_gather.15
  781.5 18.7 %reduce-scatter.12.cloned.1.call-done = bf16[896,16]{1,0:T(8,128)(2,1)} async-done(((bf16[3584,16]{1,0:T(8,128)(2,1)}), bf16[896,16]{1,0:T(8,128)(2,1)}) %reduce-scatter.12.cloned.1.call-update) | async-done | bytes 28688
  800.2 1.0 copy.23
  801.3 15.0 %all-reduce.7 = (f32[896,16]{0,1:T(8,128)}, f32[16,896]{1,0:T(8,128)}) all-reduce(f32[896,16]{0,1:T(8,128)S(1)} %convolution_bitcast_fusion.1, bf16[16,896]{1,0:T(8,128)(2,1)S(1)} %copy.23), channel_id=1, replica_groups=mesh['dp'=4,'cand'=32,'tensor'=4] {'dp'}, use_global_device_ids=true, to_apply=%region_10.11 | all-reduce | flops 28672 | bytes 200704 | tf_op jit(solution)/shard_map/psum | solution.py:114
  816.3 24.1 %all-gather.6.cloned.1.call-done = bf16[2,128,3584]{2,1,0:T(8,128)(2,1)} async-done(((bf16[2,32,3584]{2,1,0:T(8,128)(2,1)}), bf16[2,128,3584]{2,1,0:T(8,128)(2,1)}) %all-gather.6.cloned.1.call-update) | async-done | bytes 1835024 | tf_op jit(solution)/shard_map/all_gather | solution.py:94
  840.4 5.5 fusion
  845.9 1.1 fusion.12
  846.9 165.2 %all-reduce.6.cloned.1.call-done = (f32[896,16]{0,1:T(8,128)}, f32[16,896]{1,0:T(8,128)}) async-done(((f32[896,16]{0,1:T(8,128)}, f32[16,896]{1,0:T(8,128)}), (f32[896,16]{0,1:T(8,128)}, f32[16,896]{1,0:T(8,128)})) %all-reduce.6.cloned.1.call-update) | async-done | bytes 114704 | tf_op jit(solution)/shard_map/psum | solution.py:114
  1012.2 1.4 copy.31
  1013.6 1.4 copy.32
  (46 shorter events, 1.3 us)
Async XLA Ops:
  8.0 1.0 copy-start
  8.0 86.0 %all-gather.4.cloned.1.call-start = ((), (), s32[]{:S(2)}) async-start(), calls=%async_computation.3 | async-start | bytes 6623232 | tf_op jit(solution)/shard_map/all_gather | solution.py:49
  8.7 91.5 %reduce-scatter.10.cloned.1.call-start = ((), (), s32[]{:S(2)}) async-start(), calls=%async_computation.6 | async-start | bytes 40960
  10.9 121.1 %copy-start.4 = (bf16[2,32,3584]{2,1,0:T(8,128)(2,1)S(1)}, bf16[2,32,3584]{2,1,0:T(8,128)(2,1)}, u32[]{:S(2)}) copy-start(bf16[2,32,3584]{2,1,0:T(8,128)(2,1)} %param.11) | copy-start | bytes 1376260
  10.9 121.1 %copy-start.5 = (bf16[16,3584]{1,0:T(8,128)(2,1)S(1)}, bf16[16,3584]{1,0:T(8,128)(2,1)}, u32[]{:S(2)}) copy-start(bf16[16,3584]{1,0:T(8,128)(2,1)} %param.14) | copy-start | bytes 344068
  10.9 122.6 %copy-start.6 = (f32[3584]{0:T(1024)S(1)}, f32[3584]{0:T(1024)}, u32[]{:S(2)}) copy-start(f32[3584]{0:T(1024)} %param.16) | copy-start | bytes 43012
  10.9 122.6 %copy-start.7 = (f32[3584]{0:T(1024)S(1)}, f32[3584]{0:T(1024)}, u32[]{:S(2)}) copy-start(f32[3584]{0:T(1024)} %param.15) | copy-start | bytes 43012
  10.9 262.8 %copy-start.2 = (s32[2,128,1024]{2,1,0:T(8,128)S(1)}, s32[2,128,1024]{2,1,0:T(8,128)}, u32[]{:S(2)}) copy-start(s32[2,128,1024]{2,1,0:T(8,128)} %param.18) | copy-start | bytes 3145732
  11.0 262.8 %copy-start.3 = (bf16[2,128,1024]{2,1,0:T(8,128)(2,1)S(1)}, bf16[2,128,1024]{2,1,0:T(8,128)(2,1)}, u32[]{:S(2)}) copy-start(bf16[2,128,1024]{2,1,0:T(8,128)(2,1)} %param.17) | copy-start | bytes 1572868
  11.0 121.0 %reduce-scatter.8.cloned.1.call-start = ((), (), s32[]{:S(2)}) async-start(), calls=%async_computation.4 | async-start | bytes 2293760 | tf_op jit(solution)/shard_map/reduce_scatter | solution.py:53
  100.2 700.1 %reduce-scatter.12.cloned.1.call-start = ((), (), s32[]{:S(2)}) async-start(), calls=%async_computation.7 | async-start | bytes 1146880
  133.5 634.9 %copy-start.9 = (bf16[2,32,16]{1,2,0:T(8,128)(2,1)S(1)}, bf16[2,32,16]{1,2,0:T(8,128)(2,1)}, u32[]{:S(2)}) copy-start(bf16[2,32,16]{1,2,0:T(8,128)(2,1)} %copy.21) | copy-start | bytes 6148
  768.4 1.7 copy-start.1
  770.0 70.4 %all-gather.6.cloned.1.call-start = ((), (), s32[]{:S(2)}) async-start(), calls=%async_computation.5 | async-start | bytes 2293760 | tf_op jit(solution)/shard_map/all_gather | solution.py:94
  770.7 241.5 %all-reduce.6.cloned.1.call-start = ((), (), s32[]{:S(2)}) async-start(), calls=%async_computation.8 | async-start | bytes 229376 | tf_op jit(solution)/shard_map/psum | solution.py:114
  816.3 29.6 %copy-start.8 = (bf16[896,16]{0,1:T(8,128)(2,1)S(1)}, bf16[896,16]{0,1:T(8,128)(2,1)}, u32[]{:S(2)}) copy-start(bf16[896,16]{0,1:T(8,128)(2,1)} %param.13) | copy-start | bytes 86020
Sparse Core Ops, SparseCore 0:
  11.2 82.7 all-gather.3
  816.4 195.7 all-reduce.5
Sparse Core Ops, SparseCore 1:
  12.6 31.5 reduce-scatter.9
  100.3 31.7 reduce-scatter.7
  770.0 30.2 reduce-scatter.11
  803.2 37.2 all-gather.5
